TPU v7x, 128 devices: a whole 4x4x4 slice. The times are simulated.
128 devices in a mesh: tm: 4 (over y_hi, core), stn: 32 (over z, x, y_lo).
Axes of the slice: x: 4, y: 4 (y_hi: 2, y_lo: 2; y = y_hi * 2 + y_lo), z: 4, core: 2. Of those that a mesh axis runs over, the one named last changes fastest.
Arguments:
- voltages: bfloat16 [1024, 524288], P('stn', 'tm'), may hold values from -6 to 6
- delays: int32 [1024], P('stn'), may hold values from 0 to 511
- phases: int32 [1024], P('stn'), may hold values from 0 to 32767
- flags: int32 [1024], P('stn'), may hold values 0 or 1
Outputs:
- visibility: float32 [512, 1024, 1024], P(('tm', 'stn'))
All inputs are finite; a program needn't handle non-finite values. No bound on the sum of `flags` on one device may be relied on, other than what follows from the above.
Results may differ from a plain program's by a relative error of at most 0.0038.
Values may be sent and summed in bfloat16 or wider, within the bound.
No kernel may reach another device: no remote copies, remote signals or barrier semaphores. Data moves between devices by JAX's collectives and lax.ppermute only.
A program may use at most 192 MiB of HBM per device.

v0:
```python
import math

import jax
import jax.numpy as jnp
import numpy as np
from jax import lax
from jax.experimental import pallas as pl
from jax.experimental.pallas import tpu as pltpu
from jax.sharding import PartitionSpec as P

NFFT = 512
TAPS = 4
NFINE = 64
AVG = 4
BANDS = 32
STN = 32
SPEC = 4
FRAMES = SPEC * NFINE
RIM = (TAPS - 1) * NFFT
CHUNK = 16
TURN = NFFT * NFINE
F32 = jnp.float32
BF16 = jnp.bfloat16


def split_two(table):
    high = table.astype(jnp.bfloat16)
    low = (table - high.astype(np.float64)).astype(jnp.bfloat16)
    return high, low


def coarse_weights():
    length = TAPS * NFFT
    places = np.arange(length, dtype=np.float64)
    offsets = (places - length / 2 + 0.5) / NFFT
    taper = 0.54 - 0.46 * np.cos(2.0 * math.pi * places / (length - 1))
    window = (np.sinc(offsets) * taper).reshape(TAPS, NFFT)
    product = (np.arange(NFFT)[:, None] * (np.arange(BANDS) + 1)[None, :]) % NFFT
    angles = product * (2.0 * math.pi / NFFT)
    table = np.concatenate([np.cos(angles), -np.sin(angles)], 1) / math.sqrt(NFFT)
    taps = [np.concatenate(split_two(window[t][:, None] * table), 1) for t in range(TAPS)]
    return np.block([[taps[0], taps[1]], [taps[2], taps[3]]])


def fine_weights():
    product = (np.arange(NFINE)[:, None] * (np.arange(NFINE) - NFINE // 2)[None, :]) % NFINE
    angles = product * (2.0 * math.pi / NFINE)
    cosine = np.cos(angles) / math.sqrt(NFINE)
    sine = np.sin(angles) / math.sqrt(NFINE)
    full = np.zeros((2, 2, 2, NFINE, 4, 2, 4, 4, SPEC))
    pair = {(0, 0): cosine, (0, 1): -sine, (1, 0): sine, (1, 1): cosine}
    for (part_in, part_out), table in pair.items():
        for p in range(SPEC):
            full[p % 2, part_in, p // 2, :, :, part_out, :, :, p] = table.reshape(NFINE, 4, 4, 4)
    high, low = split_two(full.reshape(8 * NFINE, 512))
    return np.concatenate([high, low], 0)


def channel_kernel(
    volt_hbm, rim_hbm, w_ref, g_ref, ac_ref, as_ref, bc_ref, bs_ref, out_ref, xbuf, cbuf, dbuf, sems
):
    def copy(c):
        width = CHUNK * NFFT
        return pltpu.make_async_copy(
            volt_hbm.at[:, pl.ds(c * width, width)], xbuf.at[:, pl.ds(c * width, width)], sems.at[c]
        )

    rim_copy = pltpu.make_async_copy(
        rim_hbm, xbuf.at[:, pl.ds(FRAMES * NFFT, RIM)], sems.at[16]
    )
    for c in (0, 1, 4, 5, 2, 6, 3, 7, 8, 9, 12, 13, 10, 14, 11, 15):
        copy(c).start()
    rim_copy.start()
    lane = lax.broadcasted_iota(jnp.int32, (CHUNK * STN, 128), 1)
    first_half = lane < 64

    def spectrum(base):
        def frame(j):
            return xbuf[:, pl.ds(pl.multiple_of((base + j) * NFFT, NFFT), NFFT)]

        frames = [frame(j) for j in range(CHUNK + 3)]
        left = jnp.concatenate(frames[: CHUNK + 1], 0)
        right = jnp.concatenate(frames[2:], 0)
        both = jnp.concatenate([left, right], 1)
        z = jnp.dot(both, w_ref[...], preferred_element_type=F32)
        y = z[: CHUNK * STN, :128] + z[STN:, 128:]
        return y + pltpu.roll(y, 64, 1)

    @pl.loop(0, 8)
    def _(i):
        half = i // 4
        part = i % 4
        a = half * 8 + part

        @pl.when(i == 0)
        def _():
            copy(0).wait()

        @pl.when(part == 0)
        def _():
            copy(a + 4).wait()

        @pl.when(part < 3)
        def _():
            copy(a + 1).wait()

        @pl.when(i < 7)
        def _():
            copy(a + 5).wait()

        @pl.when(i == 7)
        def _():
            rim_copy.wait()

        s0 = spectrum(a * CHUNK)
        s1 = spectrum((a + 4) * CHUNK)
        value = jnp.where(first_half, s0, s1)
        other = jnp.where(first_half, pltpu.roll(s0, 32, 1), pltpu.roll(s1, 32, 1))
        cosine = jnp.concatenate([ac_ref[...]] * CHUNK, 0)
        sine = jnp.concatenate([as_ref[...]] * CHUNK, 0)
        row = pl.multiple_of(i * CHUNK * STN, CHUNK * STN)
        cbuf[pl.ds(row, CHUNK * STN), :] = value * cosine + other * sine

    for s in range(STN):
        turned = cbuf[pl.ds(s, 2 * NFINE, stride=STN), :].T
        dbuf[pl.ds(s, 128, stride=STN), :] = turned

    weights = jnp.concatenate([g_ref[:512, :], g_ref[:512, :], g_ref[512:, :]], 0)
    rows = 512

    for h in range(1024 // rows):
        data = jnp.concatenate([dbuf[x * 1024 + h * rows : x * 1024 + (h + 1) * rows, :] for x in range(4)], 1)
        high = data.astype(BF16)
        low = (data - high.astype(F32)).astype(BF16)
        z = jnp.dot(jnp.concatenate([high, low, high], 1), weights, preferred_element_type=F32)
        per = rows // STN
        for kh in range(4):
            piece = z[:, kh * 128 : (kh + 1) * 128]
            cosine = jnp.concatenate([bc_ref[:, kh * 128 : (kh + 1) * 128]] * per, 0)
            sine = jnp.concatenate([bs_ref[:, kh * 128 : (kh + 1) * 128]] * per, 0)
            result = (piece * cosine + pltpu.roll(piece, 64, 1) * sine).astype(BF16)
            for j in range(per):
                out_ref[(h * per + j) * 4 + kh] = result[j * STN : (j + 1) * STN]


def channelize(voltages, rim, ac, asn, bc, bs):
    vm = pl.BlockSpec(memory_space=pltpu.VMEM)
    hbm = pl.BlockSpec(memory_space=pl.ANY)
    return pl.pallas_call(
        channel_kernel,
        out_shape=jax.ShapeDtypeStruct((128, STN, 128), BF16),
        in_specs=[hbm, hbm, vm, vm, vm, vm, vm, vm],
        out_specs=vm,
        scratch_shapes=[
            pltpu.VMEM((STN, FRAMES * NFFT + RIM), BF16),
            pltpu.VMEM((2 * NFINE * STN, 128), F32),
            pltpu.VMEM((128 * STN, 128), F32),
            pltpu.SemaphoreType.DMA((17,)),
        ],
        name="channelize",
    )(voltages, rim, jnp.asarray(coarse_weights()), jnp.asarray(fine_weights()), ac, asn, bc, bs)


def correlate_kernel(r_ref, out_ref, x_buf, s_buf):
    group = pl.program_id(0)
    block = pl.program_id(1)

    for g in range(4):

        @pl.when((block == 0) & (group == g))
        def _():
            rows = 256
            lane = lax.broadcasted_iota(jnp.int32, (rows, 128), 1)
            place = (lane // 16) % 4
            sign = jnp.where(lane < 64, -1.0, 1.0)
            for n in range(1024 // rows):
                value = None
                for t in range(4):
                    start = t * 32 + n * rows // STN
                    src = r_ref[start : start + rows // STN].reshape(rows, 128).astype(F32)
                    shift = (16 * (t - g)) % 128
                    moved = pltpu.roll(src, shift, 1) if shift else src
                    value = moved if value is None else jnp.where(place == t, moved, value)
                x_buf[n * rows : (n + 1) * rows, :] = value.astype(BF16)
                s_buf[n * rows : (n + 1) * rows, :] = (pltpu.roll(value, 64, 1) * sign).astype(BF16)

    def product(left, right):
        return lax.dot_general(left, right, (((1,), (1,)), ((), ())), preferred_element_type=F32)

    for i in range(4):

        @pl.when(block == i)
        def _():
            mine = x_buf[i * 256 : (i + 1) * 256, :]
            if i > 0:
                out_ref[0, :, : i * 256] = product(mine, s_buf[: i * 256, :])
            if i < 3:
                out_ref[0, :, (i + 1) * 256 :] = product(mine, x_buf[(i + 1) * 256 :, :])
            real = product(mine, mine)
            imag = product(mine, s_buf[i * 256 : (i + 1) * 256, :])
            row = lax.broadcasted_iota(jnp.int32, (256, 256), 0)
            col = lax.broadcasted_iota(jnp.int32, (256, 256), 1)
            out_ref[0, :, i * 256 : (i + 1) * 256] = jnp.where(col >= row, real, imag)


def correlate(received):
    return pl.pallas_call(
        correlate_kernel,
        out_shape=jax.ShapeDtypeStruct((4, 1024, 1024), F32),
        grid=(4, 4),
        in_specs=[pl.BlockSpec(memory_space=pltpu.VMEM)],
        out_specs=pl.BlockSpec((1, 256, 1024), lambda g, i: (g, i, 0)),
        scratch_shapes=[pltpu.VMEM((1024, 128), BF16), pltpu.VMEM((1024, 128), BF16)],
        name="correlate",
    )(received)


def rotations(delays, phases, flags):
    def turn(index):
        angles = jnp.mod(index, TURN).astype(F32) * (-2.0 * math.pi / TURN)
        return jnp.cos(angles), jnp.sin(angles)

    lane = jnp.arange(128, dtype=jnp.int32)[None, :]
    band = lane % 32
    sign = jnp.where((lane // 32) % 2 == 0, -1.0, 1.0)
    cosine, sine = turn(delays[:, None] * ((band + 1) * NFINE) + phases[:, None])
    keep = flags.astype(F32)[:, None] * 0.125
    ac = cosine * keep
    asn = sine * keep * sign
    lane = jnp.arange(512, dtype=jnp.int32)[None, :]
    fine_id = (lane // 128) * 16 + (lane % 64) // 4
    sign = jnp.where((lane // 64) % 2 == 0, -1.0, 1.0)
    bc, sine = turn(delays[:, None] * (fine_id - NFINE // 2))
    return ac, asn, bc, sine * sign


def local(voltages, delays, phases, flags):
    rim = lax.ppermute(voltages[:, :RIM], "tm", [(1, 0), (2, 1), (3, 2)])
    sent = channelize(voltages, rim, *rotations(delays, phases, flags))
    received = lax.all_to_all(sent, ("tm", "stn"), 0, 0, tiled=True)
    return correlate(received)


def solution(mesh):
    in_specs = (P("stn", "tm"), P("stn"), P("stn"), P("stn"))
    out_specs = P(("tm", "stn"), None, None)
    return jax.shard_map(local, mesh=mesh, in_specs=in_specs, out_specs=out_specs, check_vma=False)
```

profile of v0, /device:TPU:1, one launch (start us, length us, event | category | flops | bytes accessed | tf_op | source)
XLA Modules:
  0.0 69.2 jit_solution(606719378465183502)
XLA Ops:
  0.0 0.9 %slice.3 = bf16[32,1536]{1,0:T(8,128)(2,1)S(1)} slice(bf16[32,131072]{1,0:T(8,128)(2,1)} %volt_hbm.1), slice={[0:32], [0:1536]} | slice | bytes 196608 | tf_op jit(solution)/shard_map/slice | solution.py:238
  0.9 3.3 %collective-permute-start = (bf16[32,1536]{1,0:T(8,128)(2,1)S(1)}, bf16[32,1536]{1,0:T(8,128)(2,1)S(1)}, u32[]{:S(2)}, u32[]{:S(2)}) collective-permute-start(bf16[32,1536]{1,0:T(8,128)(2,1)S(1)} %slice.3), channel_id=1, source_target_pairs={{32,0},{64,32},{96,64},{33,1},{65,33},{97,65},{34,2},{66,34},{98,6... | collective-permute-start | bytes 294920 | tf_op jit(solution)/shard_map/ppermute | solution.py:238
  4.2 0.7 convert_multiply_fusion
  4.9 1.6 %sine_multiply_fusion = (f32[32,512]{1,0:T(8,128)}, f32[32,512]{1,0:T(8,128)}) fusion(f32[512]{0:T(512)S(1)} %fusion.22, s32[512]{0:T(512)S(1)} %fusion.13, s32[32]{0:T(128)} %param.7), kind=kLoop, calls=%fused_computation.8 | loop fusion | flops 245760 | bytes 135296 | tf_op jit(solution)/shard_map/mul | solution.py:234
  6.5 1.4 %multiply_multiply_fusion = (f32[32,128]{1,0:T(8,128)}, f32[32,128]{1,0:T(8,128)}) fusion(f32[128]{0:T(128)S(1)} %compare_select_fusion.2, f32[32]{0:T(128)S(1)} %convert_multiply_fusion, s32[32]{0:T(128)} %param.8, s32[128]{0:T(128)S(1)} %fusion.24, s32[32]{0:T(128)} %param.7), kind=kLoop, calls=%fused_computation.16 | loop fusion | flops 73728 | bytes 34176 | tf_op jit(solution)/shard_map/mul | solution.py:229
  8.0 1.4 %collective-permute-done.rim_hbm = bf16[32,1536]{1,0:T(8,128)(2,1)S(1)} collective-permute-done((bf16[32,1536]{1,0:T(8,128)(2,1)S(1)}, bf16[32,1536]{1,0:T(8,128)(2,1)S(1)}, u32[]{:S(2)}, u32[]{:S(2)}) %collective-permute-start) | collective-permute-done | bytes 98336 | tf_op jit(solution)/shard_map/ppermute | solution.py:238
  9.4 0.0 copy-start
  9.4 0.6 copy-done
  10.0 16.1 %channelize.1 = bf16[128,32,128]{2,1,0:T(8,128)(2,1)} custom-call(bf16[32,131072]{1,0:T(8,128)(2,1)} %volt_hbm.1, bf16[32,1536]{1,0:T(8,128)(2,1)} %copy-done, bf16[1024,256]{1,0:T(8,128)(2,1)} %constant.141.clone.w_ref, bf16[1024,512]{1,0:T(8,128)(2,1)} %constant.142.clone.g_ref, f32[32,128]{1,0:T(8,128)} %get-tuple-element.8.ac_ref, ...), custom_call_target="tpu_custom_call" | custom-call | tf_op jit(solution)/shard_map/channelize/pallas_call | solution.py:149
  26.1 28.8 %all_to_all.5.r_ref = bf16[128,32,128]{2,1,0:T(8,128)(2,1)} all-to-all(bf16[128,32,128]{2,1,0:T(8,128)(2,1)} %channelize.1), channel_id=1, replica_groups=mesh['tm'=4,'stn'=32] {'tm','stn'}, dimensions={0} | all-to-all | bytes 2097152 | tf_op jit(solution)/shard_map/all_to_all | solution.py:240
  54.9 14.3 %correlate.1 = f32[4,1024,1024]{2,1,0:T(8,128)} custom-call(bf16[128,32,128]{2,1,0:T(8,128)(2,1)} %all_to_all.5.r_ref), custom_call_target="tpu_custom_call" | custom-call | tf_op jit(solution)/shard_map/correlate/pallas_call | solution.py:207
  (4 shorter events, 0.0 us)
Async XLA Ops:
  0.9 8.5 %collective-permute-start = (bf16[32,1536]{1,0:T(8,128)(2,1)S(1)}, bf16[32,1536]{1,0:T(8,128)(2,1)S(1)}, u32[]{:S(2)}, u32[]{:S(2)}) collective-permute-start(bf16[32,1536]{1,0:T(8,128)(2,1)S(1)} %slice.3), channel_id=1, source_target_pairs={{32,0},{64,32},{96,64},{33,1},{65,33},{97,65},{34,2},{66,34},{98,6... | collective-permute-start | bytes 294920 | tf_op jit(solution)/shard_map/ppermute | solution.py:238
  9.4 0.6 copy-start
where the time goes:
time: 69.5 us; the launch traced here: 69.2 us
  Pallas kernels  30.4 us (44%)
  blocking collectives  28.8 us (41%)
  other arithmetic  3.77 us (5%)
  starting transfers between devices  3.28 us (5%)
  local copies, waits for them, and re-layouts  1.52 us (2%)
  waiting for transfers between devices  1.4 us (2%)
    all_to_all x1, blocking collectives, local(): received = lax.all_to_all(sent, ('tm', 'stn'), 0, 0, tiled=True)  28.8 us
    pallas_call x1, Pallas kernels, channelize(): pl.pallas_call(channel_kernel, out_shape=jax.ShapeDtypeStruct((128, STN,...  16.1 us
    pallas_call x1, Pallas kernels, correlate(): pl.pallas_call(correlate_kernel, out_shape=jax.ShapeDtypeStruct((4, 1024,...  14.3 us
    ppermute x1, starting transfers between devices, local(): rim = lax.ppermute(voltages[:, :RIM], 'tm', [(1, 0), (2, 1), (3, 2)])  3.28 us
    mul x1, other arithmetic, rotations(): return (ac, asn, bc, sine * sign)  1.64 us
    mul x1, other arithmetic, rotations(): asn = sine * keep * sign  1.44 us
    ppermute x1, waiting for transfers between devices, local(): rim = lax.ppermute(voltages[:, :RIM], 'tm', [(1, 0), (2, 1), (3, 2)])  1.4 us
  transfers between devices with their start and end apart: 1, of which 1 were waited for; matrix products, arithmetic and copies ran while one was open for 5% of the time, Pallas kernels for 0%

commit v1 on v0

--- a/solution.py
+++ b/solution.py
@@ -161,56 +161,71 @@
     )(voltages, rim, jnp.asarray(coarse_weights()), jnp.asarray(fine_weights()), ac, asn, bc, bs)
 
 
-def correlate_kernel(r_ref, out_ref, x_buf, s_buf):
-    group = pl.program_id(0)
-    block = pl.program_id(1)
-
-    for g in range(4):
-
-        @pl.when((block == 0) & (group == g))
-        def _():
-            rows = 256
-            lane = lax.broadcasted_iota(jnp.int32, (rows, 128), 1)
-            place = (lane // 16) % 4
-            sign = jnp.where(lane < 64, -1.0, 1.0)
-            for n in range(1024 // rows):
-                value = None
-                for t in range(4):
-                    start = t * 32 + n * rows // STN
-                    src = r_ref[start : start + rows // STN].reshape(rows, 128).astype(F32)
-                    shift = (16 * (t - g)) % 128
-                    moved = pltpu.roll(src, shift, 1) if shift else src
-                    value = moved if value is None else jnp.where(place == t, moved, value)
-                x_buf[n * rows : (n + 1) * rows, :] = value.astype(BF16)
-                s_buf[n * rows : (n + 1) * rows, :] = (pltpu.roll(value, 64, 1) * sign).astype(BF16)
+def correlate_kernel(r_ref, out_hbm, x_buf, s_buf, o_buf, sems):
+    rows = 128
+    lane = lax.broadcasted_iota(jnp.int32, (rows, 128), 1)
+    place = (lane // 16) % 4
+    sign = jnp.where(lane < 64, -1.0, 1.0)
+
+    def prepare(g, n):
+        slot = g % 2
+        value = None
+        for t in range(4):
+            start = t * 32 + n * rows // STN
+            src = r_ref[start : start + rows // STN].reshape(rows, 128).astype(F32)
+            shift = (16 * (t - g)) % 128
+            moved = pltpu.roll(src, shift, 1) if shift else src
+            value = moved if value is None else jnp.where(place == t, moved, value)
+        x_buf[slot, n * rows : (n + 1) * rows, :] = value.astype(BF16)
+        s_buf[slot, n * rows : (n + 1) * rows, :] = (pltpu.roll(value, 64, 1) * sign).astype(BF16)
 
     def product(left, right):
         return lax.dot_general(left, right, (((1,), (1,)), ((), ())), preferred_element_type=F32)
 
-    for i in range(4):
-
-        @pl.when(block == i)
-        def _():
-            mine = x_buf[i * 256 : (i + 1) * 256, :]
-            if i > 0:
-                out_ref[0, :, : i * 256] = product(mine, s_buf[: i * 256, :])
-            if i < 3:
-                out_ref[0, :, (i + 1) * 256 :] = product(mine, x_buf[(i + 1) * 256 :, :])
-            real = product(mine, mine)
-            imag = product(mine, s_buf[i * 256 : (i + 1) * 256, :])
-            row = lax.broadcasted_iota(jnp.int32, (256, 256), 0)
-            col = lax.broadcasted_iota(jnp.int32, (256, 256), 1)
-            out_ref[0, :, i * 256 : (i + 1) * 256] = jnp.where(col >= row, real, imag)
+    def send(g, j):
+        cols = pl.ds(j * 256, 256)
+        return pltpu.make_async_copy(
+            o_buf.at[g % 2, :, cols], out_hbm.at[g, :, cols], sems.at[g % 2, j]
+        )
+
+    row = lax.broadcasted_iota(jnp.int32, (256, 256), 0)
+    upper = lax.broadcasted_iota(jnp.int32, (256, 256), 1) >= row
+    for n in range(8):
+        prepare(0, n)
+    for g in range(4):
+        slot = g % 2
+        for j in range(4):
+            low, high = j * 256, (j + 1) * 256
+            if g >= 2:
+                send(g - 2, j).wait()
+            if g < 3:
+                prepare(g + 1, 2 * j)
+                prepare(g + 1, 2 * j + 1)
+            real = product(x_buf[slot, :high, :], x_buf[slot, low:high, :])
+            imag = product(x_buf[slot, low:, :], s_buf[slot, low:high, :])
+            if j > 0:
+                o_buf[slot, :low, low:high] = real[:low]
+            if j < 3:
+                o_buf[slot, high:, low:high] = imag[256:]
+            o_buf[slot, low:high, low:high] = jnp.where(upper, real[low:], imag[:256])
+            send(g, j).start()
+    for g in (2, 3):
+        for j in range(4):
+            send(g, j).wait()
 
 
 def correlate(received):
     return pl.pallas_call(
         correlate_kernel,
         out_shape=jax.ShapeDtypeStruct((4, 1024, 1024), F32),
-        grid=(4, 4),
         in_specs=[pl.BlockSpec(memory_space=pltpu.VMEM)],
-        out_specs=pl.BlockSpec((1, 256, 1024), lambda g, i: (g, i, 0)),
-        scratch_shapes=[pltpu.VMEM((1024, 128), BF16), pltpu.VMEM((1024, 128), BF16)],
+        out_specs=pl.BlockSpec(memory_space=pl.ANY),
+        scratch_shapes=[
+            pltpu.VMEM((2, 1024, 128), BF16),
+            pltpu.VMEM((2, 1024, 128), BF16),
+            pltpu.VMEM((2, 1024, 1024), F32),
+            pltpu.SemaphoreType.DMA((2, 4)),
+        ],
         name="correlate",
     )(received)
 

time: 69.5 us -> 63.3 us (0.911)
  Pallas kernels: 30.4 us -> 24.2 us
    pallas_call x1, Pallas kernels: 14.3 us -> 8.15 us  [correlate(): pl.pallas_call(correlate_kernel, out_shape=jax.ShapeDtypeStruct((4, 1024,...]
  transfers between devices with their start and end apart: 1 -> 1, of which waited for: 1 -> 1; matrix products, arithmetic and copies ran while one was open for 5% -> 6% of each run, Pallas kernels for 0% -> 0%
where the time goes in v1:
time: 63.3 us; the launch traced here: 63 us
  blocking collectives  28.8 us (45%)
  Pallas kernels  24.2 us (38%)
  other arithmetic  3.77 us (6%)
  starting transfers between devices  3.28 us (5%)
  local copies, waits for them, and re-layouts  1.52 us (2%)
  waiting for transfers between devices  1.4 us (2%)
    all_to_all x1, blocking collectives, local(): received = lax.all_to_all(sent, ('tm', 'stn'), 0, 0, tiled=True)  28.8 us
    pallas_call x1, Pallas kernels, channelize(): pl.pallas_call(channel_kernel, out_shape=jax.ShapeDtypeStruct((128, STN,...  16.1 us
    pallas_call x1, Pallas kernels, correlate(): pl.pallas_call(correlate_kernel, out_shape=jax.ShapeDtypeStruct((4, 1024,...  8.15 us
    ppermute x1, starting transfers between devices, local(): rim = lax.ppermute(voltages[:, :RIM], 'tm', [(1, 0), (2, 1), (3, 2)])  3.28 us
    mul x1, other arithmetic, rotations(): return (ac, asn, bc, sine * sign)  1.64 us
    mul x1, other arithmetic, rotations(): asn = sine * keep * sign  1.44 us
    ppermute x1, waiting for transfers between devices, local(): rim = lax.ppermute(voltages[:, :RIM], 'tm', [(1, 0), (2, 1), (3, 2)])  1.4 us
  transfers between devices with their start and end apart: 1, of which 1 were waited for; matrix products, arithmetic and copies ran while one was open for 6% of the time, Pallas kernels for 0%

profile of v1, /device:TPU:1, one launch (start us, length us, event | category | flops | bytes accessed | tf_op | source)
XLA Modules:
  0.0 63.0 jit_solution(12195592160389499927)
XLA Ops:
  0.0 0.9 %slice.3 = bf16[32,1536]{1,0:T(8,128)(2,1)S(1)} slice(bf16[32,131072]{1,0:T(8,128)(2,1)} %volt_hbm.1), slice={[0:32], [0:1536]} | slice | bytes 196608 | tf_op jit(solution)/shard_map/slice | solution.py:253
  0.9 3.3 %collective-permute-start = (bf16[32,1536]{1,0:T(8,128)(2,1)S(1)}, bf16[32,1536]{1,0:T(8,128)(2,1)S(1)}, u32[]{:S(2)}, u32[]{:S(2)}) collective-permute-start(bf16[32,1536]{1,0:T(8,128)(2,1)S(1)} %slice.3), channel_id=1, source_target_pairs={{32,0},{64,32},{96,64},{33,1},{65,33},{97,65},{34,2},{66,34},{98,6... | collective-permute-start | bytes 294920 | tf_op jit(solution)/shard_map/ppermute | solution.py:253
  4.2 0.7 %convert_multiply_fusion = f32[32]{0:T(128)S(1)} fusion(s32[32]{0:T(128)} %param.9), kind=kLoop, calls=%fused_computation.59 | loop fusion | flops 64 | bytes 256 | tf_op jit(solution)/shard_map/mul | solution.py:242
  4.9 1.6 %sine_multiply_fusion = (f32[32,512]{1,0:T(8,128)}, f32[32,512]{1,0:T(8,128)}) fusion(f32[512]{0:T(512)S(1)} %fusion.22, s32[512]{0:T(512)S(1)} %fusion.13, s32[32]{0:T(128)} %param.7), kind=kLoop, calls=%fused_computation.8 | loop fusion | flops 245760 | bytes 135296 | tf_op jit(solution)/shard_map/mul | solution.py:249
  6.5 1.4 %multiply_multiply_fusion = (f32[32,128]{1,0:T(8,128)}, f32[32,128]{1,0:T(8,128)}) fusion(f32[128]{0:T(128)S(1)} %compare_select_fusion.2, f32[32]{0:T(128)S(1)} %convert_multiply_fusion, s32[32]{0:T(128)} %param.8, s32[128]{0:T(128)S(1)} %fusion.24, s32[32]{0:T(128)} %param.7), kind=kLoop, calls=%fused_computation.16 | loop fusion | flops 73728 | bytes 34176 | tf_op jit(solution)/shard_map/mul | solution.py:244
  8.0 1.4 %collective-permute-done.rim_hbm = bf16[32,1536]{1,0:T(8,128)(2,1)S(1)} collective-permute-done((bf16[32,1536]{1,0:T(8,128)(2,1)S(1)}, bf16[32,1536]{1,0:T(8,128)(2,1)S(1)}, u32[]{:S(2)}, u32[]{:S(2)}) %collective-permute-start) | collective-permute-done | bytes 98336 | tf_op jit(solution)/shard_map/ppermute | solution.py:253
  9.4 0.0 copy-start
  9.4 0.6 copy-done
  10.0 16.1 %channelize.1 = bf16[128,32,128]{2,1,0:T(8,128)(2,1)} custom-call(bf16[32,131072]{1,0:T(8,128)(2,1)} %volt_hbm.1, bf16[32,1536]{1,0:T(8,128)(2,1)} %copy-done, bf16[1024,256]{1,0:T(8,128)(2,1)} %constant.141.clone.w_ref, bf16[1024,512]{1,0:T(8,128)(2,1)} %constant.142.clone.g_ref, f32[32,128]{1,0:T(8,128)} %get-tuple-element.8.ac_ref, ...), custom_call_target="tpu_custom_call" | custom-call | tf_op jit(solution)/shard_map/channelize/pallas_call | solution.py:149
  26.1 28.8 %all_to_all.5.r_ref = bf16[128,32,128]{2,1,0:T(8,128)(2,1)} all-to-all(bf16[128,32,128]{2,1,0:T(8,128)(2,1)} %channelize.1), channel_id=1, replica_groups=mesh['tm'=4,'stn'=32] {'tm','stn'}, dimensions={0} | all-to-all | bytes 2097152 | tf_op jit(solution)/shard_map/all_to_all | solution.py:255
  54.9 8.1 %correlate.1 = f32[4,1024,1024]{2,1,0:T(8,128)} custom-call(bf16[128,32,128]{2,1,0:T(8,128)(2,1)} %all_to_all.5.r_ref), custom_call_target="tpu_custom_call" | custom-call | tf_op jit(solution)/shard_map/correlate/pallas_call | solution.py:218
  (4 shorter events, 0.0 us)
Async XLA Ops:
  0.9 8.5 %collective-permute-start = (bf16[32,1536]{1,0:T(8,128)(2,1)S(1)}, bf16[32,1536]{1,0:T(8,128)(2,1)S(1)}, u32[]{:S(2)}, u32[]{:S(2)}) collective-permute-start(bf16[32,1536]{1,0:T(8,128)(2,1)S(1)} %slice.3), channel_id=1, source_target_pairs={{32,0},{64,32},{96,64},{33,1},{65,33},{97,65},{34,2},{66,34},{98,6... | collective-permute-start | bytes 294920 | tf_op jit(solution)/shard_map/ppermute | solution.py:253
  9.4 0.6 copy-start

commit v2 on v1

v2 whole, which is shorter than its diff:
```python
import math

import jax
import jax.numpy as jnp
import numpy as np
from jax import lax
from jax.experimental import pallas as pl
from jax.experimental.pallas import tpu as pltpu
from jax.sharding import PartitionSpec as P

NFFT = 512
TAPS = 4
NFINE = 64
AVG = 4
BANDS = 32
STN = 32
SPEC = 4
FRAMES = SPEC * NFINE
RIM = (TAPS - 1) * NFFT
CHUNK = 16
WIDE = 32
TURN = NFFT * NFINE
F32 = jnp.float32
BF16 = jnp.bfloat16


def split_two(table):
    high = table.astype(jnp.bfloat16)
    low = (table - high.astype(np.float64)).astype(jnp.bfloat16)
    return high, low


def coarse_weights():
    length = TAPS * NFFT
    places = np.arange(length, dtype=np.float64)
    offsets = (places - length / 2 + 0.5) / NFFT
    taper = 0.54 - 0.46 * np.cos(2.0 * math.pi * places / (length - 1))
    window = (np.sinc(offsets) * taper).reshape(TAPS, NFFT)
    product = (np.arange(NFFT)[:, None] * (np.arange(BANDS) + 1)[None, :]) % NFFT
    angles = product * (2.0 * math.pi / NFFT)
    table = np.concatenate([np.cos(angles), -np.sin(angles)], 1) / math.sqrt(NFFT)
    taps = [np.concatenate(split_two(window[t][:, None] * table), 1) for t in range(TAPS)]
    return np.block([[taps[0], taps[1]], [taps[2], taps[3]]])


def fine_weights():
    product = (np.arange(NFINE)[:, None] * (np.arange(NFINE) - NFINE // 2)[None, :]) % NFINE
    angles = product * (2.0 * math.pi / NFINE)
    cosine = np.cos(angles) / math.sqrt(NFINE)
    sine = np.sin(angles) / math.sqrt(NFINE)
    full = np.zeros((2, 2, NFINE, 2, NFINE, 2))
    pair = {(0, 0): cosine, (0, 1): -sine, (1, 0): sine, (1, 1): cosine}
    for (part_in, part_out), table in pair.items():
        for p in range(2):
            full[part_in, p, :, part_out, :, p] = table
    high, low = split_two(full.reshape(4 * NFINE, 4 * NFINE))
    return np.concatenate([high, high, low], 0)


def send_moves():
    source = np.arange(512).reshape(4, 4, 32).transpose(1, 0, 2).reshape(-1)
    return np.eye(512)[:, source].astype(jnp.bfloat16)


def group_moves():
    source = np.arange(512).reshape(4, 2, 2, 4, 8).transpose(3, 1, 2, 0, 4).reshape(-1)
    return np.eye(512)[:, source].astype(jnp.bfloat16)


def channel_kernel(
    volt_hbm, rim_ref, w_ref, g_ref, m_ref, d_ref, p_ref, f_ref, out_ref, xbuf, cbuf, dbuf, tcos, tsin, sems
):
    def copy(c):
        width = CHUNK * NFFT
        return pltpu.make_async_copy(
            volt_hbm.at[:, pl.ds(c * width, width)], xbuf.at[:, pl.ds(c * width, width)], sems.at[c]
        )

    for c in (0, 1, 4, 5, 2, 6, 3, 7, 8, 9, 12, 13, 10, 14, 11, 15):
        copy(c).start()
    xbuf[:, FRAMES * NFFT :] = rim_ref[...]
    first_half = lax.broadcasted_iota(jnp.int32, (WIDE * STN, 128), 1) < 64
    diagonal = lax.broadcasted_iota(jnp.int32, (STN, STN), 0) == lax.broadcasted_iota(jnp.int32, (STN, STN), 1)

    def column(ref):
        spread = jnp.broadcast_to(ref[...].astype(F32), (STN, STN))
        picked = jnp.sum(jnp.where(diagonal, spread, 0.0), 1, keepdims=True)
        return jnp.broadcast_to(picked, (STN, 128))

    delay = column(d_ref).astype(jnp.int32)
    phase = column(p_ref).astype(jnp.int32)
    keep = column(f_ref) * 0.125
    fine_id = lax.broadcasted_iota(jnp.int32, (STN, 128), 1) // 2 - NFINE // 2

    def rotation(band):
        index = (delay * ((band + 1) * NFINE + fine_id) + phase) & (TURN - 1)
        quarter = (index + TURN // 8) >> 13
        angle = (index - (quarter << 13)).astype(F32) * (2.0 * math.pi / TURN)
        square = angle * angle
        sine = -1.9515295891e-4 * square + 8.3321608736e-3
        sine = (sine * square - 1.6666654611e-1) * square * angle + angle
        cosine = 2.443315711809948e-5 * square - 1.388731625493765e-3
        cosine = (cosine * square + 4.166664568298827e-2) * square * square - 0.5 * square + 1.0
        swap = (quarter & 1) == 1
        real = jnp.where(swap, sine, cosine) * keep
        imag = jnp.where(swap, cosine, sine) * keep
        real = jnp.where(((quarter + 1) & 2) == 2, -real, real)
        imag = jnp.where((quarter & 2) == 2, -imag, imag)
        row = pl.multiple_of(band * STN, STN)
        tcos[pl.ds(row, STN), :] = real
        tsin[pl.ds(row, STN), :] = imag

    def spectrum(base):
        def frame(j):
            return xbuf[:, pl.ds(pl.multiple_of((base + j) * NFFT, NFFT), NFFT)]

        frames = [frame(j) for j in range(WIDE + 3)]
        left = jnp.concatenate(frames[: WIDE + 1], 0)
        right = jnp.concatenate(frames[2:], 0)
        both = jnp.concatenate([left, right], 1)
        z = jnp.dot(both, w_ref[...], preferred_element_type=F32)
        return z[: WIDE * STN, :128] + z[STN:, 128:]

    @pl.loop(0, 4)
    def _(i):
        part = i % 2
        a = (i // 2) * 8 + part * 2

        @pl.when(i == 0)
        def _():
            copy(0).wait()

        @pl.when(part == 0)
        def _():
            for c in (1, 2, 4, 5, 6):
                copy(a + c).wait()

        @pl.when(part == 1)
        def _():
            for c in (1, 5):
                copy(a + c).wait()

        @pl.when(i == 1)
        def _():
            copy(8).wait()

        y0 = spectrum(a * CHUNK)
        y1 = spectrum((a + 4) * CHUNK)
        value = jnp.where(first_half, y0, y1) + pltpu.roll(jnp.where(first_half, y1, y0), 64, 1)
        cbuf[pl.ds(pl.multiple_of(i * WIDE, WIDE), WIDE)] = value.reshape(WIDE, STN, 128)
        for j in range(8):
            rotation(i * 8 + j)

    for sb in range(4):
        streams = jnp.swapaxes(cbuf[:, sb * 8 : (sb + 1) * 8, :], 0, 1)
        turned = jnp.stack([streams[s].T for s in range(8)], 0)
        dbuf[:, sb * 8 : (sb + 1) * 8, :] = jnp.swapaxes(turned, 0, 1)

    per = 16
    rows = per * STN
    for h in range(BANDS // per):
        reals, imags = [], []
        cosine = tcos[h * rows : (h + 1) * rows, :]
        sine = tsin[h * rows : (h + 1) * rows, :]
        for p in range(2):
            starts = [(p * 2 + q) * BANDS + h * per for q in range(2)]
            data = jnp.concatenate([dbuf[x : x + per].reshape(rows, 128) for x in starts], 1)
            high = data.astype(BF16)
            low = (data - high.astype(F32)).astype(BF16)
            z = jnp.dot(jnp.concatenate([high, low, high], 1), g_ref[...], preferred_element_type=F32)
            reals.append((z[:, :128] * cosine + z[:, 128:] * sine).astype(BF16))
            imags.append((z[:, 128:] * cosine - z[:, :128] * sine).astype(BF16))
        moved = jnp.dot(jnp.concatenate(reals + imags, 1), m_ref[...], preferred_element_type=F32).astype(BF16)
        for j in range(per):
            for kh in range(4):
                out_ref[(h * per + j) * 4 + kh] = moved[j * STN : (j + 1) * STN, kh * 128 : (kh + 1) * 128]


def channelize(voltages, rim, delays, phases, flags):
    vm = pl.BlockSpec(memory_space=pltpu.VMEM)
    hbm = pl.BlockSpec(memory_space=pl.ANY)
    return pl.pallas_call(
        channel_kernel,
        out_shape=jax.ShapeDtypeStruct((128, STN, 128), BF16),
        in_specs=[hbm] + [vm] * 7,
        out_specs=vm,
        scratch_shapes=[
            pltpu.VMEM((STN, FRAMES * NFFT + RIM), BF16),
            pltpu.VMEM((2 * NFINE, STN, 128), F32),
            pltpu.VMEM((128, STN, 128), F32),
            pltpu.VMEM((BANDS * STN, 128), F32),
            pltpu.VMEM((BANDS * STN, 128), F32),
            pltpu.SemaphoreType.DMA((16,)),
        ],
        name="channelize",
    )(
        voltages,
        rim,
        jnp.asarray(coarse_weights()),
        jnp.asarray(fine_weights()),
        jnp.asarray(send_moves()),
        delays.reshape(1, STN),
        phases.reshape(1, STN),
        flags.reshape(1, STN),
    )


def correlate_kernel(r_ref, m_ref, out_hbm, x_buf, s_buf, o_buf, sems):
    sign = jnp.where(lax.broadcasted_iota(jnp.int32, (1024, 128), 1) < 64, 1.0, -1.0)

    def prepare(pair):
        parts = [r_ref[t * STN : (t + 1) * STN].reshape(1024, 128) for t in range(4)]
        both = jnp.dot(
            jnp.concatenate(parts, 1), m_ref[:, pair * 256 : (pair + 1) * 256], preferred_element_type=F32
        )
        for k in range(2):
            value = both[:, k * 128 : (k + 1) * 128]
            x_buf[pair * 2 + k] = value.astype(BF16)
            s_buf[pair * 2 + k] = (pltpu.roll(value, 64, 1) * sign).astype(BF16)

    def product(left, right):
        return lax.dot_general(left, right, (((1,), (1,)), ((), ())), preferred_element_type=F32)

    def send(g, j):
        cols = pl.ds(j * 256, 256)
        return pltpu.make_async_copy(o_buf.at[g, :, cols], out_hbm.at[g, :, cols], sems.at[g, j])

    row = lax.broadcasted_iota(jnp.int32, (256, 256), 0)
    upper = lax.broadcasted_iota(jnp.int32, (256, 256), 1) >= row
    prepare(0)
    for g in range(4):
        for j in range(4):
            low, high = j * 256, (j + 1) * 256
            column = x_buf[g, low:high, :]
            real = product(x_buf[g, :high, :], column)
            imag = product(s_buf[g, low:, :], column)
            if j > 0:
                o_buf[g, :low, low:high] = real[:low]
            if j < 3:
                o_buf[g, high:, low:high] = imag[256:]
            o_buf[g, low:high, low:high] = jnp.where(upper, real[low:], imag[:256])
            send(g, j).start()
        if g == 0:
            prepare(1)
    for g in range(4):
        for j in range(4):
            send(g, j).wait()


def correlate(received):
    return pl.pallas_call(
        correlate_kernel,
        out_shape=jax.ShapeDtypeStruct((4, 1024, 1024), F32),
        in_specs=[pl.BlockSpec(memory_space=pltpu.VMEM)] * 2,
        out_specs=pl.BlockSpec(memory_space=pl.ANY),
        scratch_shapes=[
            pltpu.VMEM((4, 1024, 128), BF16),
            pltpu.VMEM((4, 1024, 128), BF16),
            pltpu.VMEM((4, 1024, 1024), F32),
            pltpu.SemaphoreType.DMA((4, 4)),
        ],
        name="correlate",
    )(received, jnp.asarray(group_moves()))


def local(voltages, delays, phases, flags):
    rim = lax.ppermute(voltages[:, :RIM], "tm", [(1, 0), (2, 1), (3, 2)])
    sent = channelize(voltages, rim, delays, phases, flags)
    received = lax.all_to_all(sent, ("tm", "stn"), 0, 0, tiled=True)
    return correlate(received)


def solution(mesh):
    in_specs = (P("stn", "tm"), P("stn"), P("stn"), P("stn"))
    out_specs = P(("tm", "stn"), None, None)
    return jax.shard_map(local, mesh=mesh, in_specs=in_specs, out_specs=out_specs, check_vma=False)
```

time: 63.3 us -> 58.7 us (0.927)
  waiting for transfers between devices: 1.4 us -> 5.2 us
  other arithmetic: 3.77 us -> 0 us
  Pallas kernels: 24.2 us -> 20.6 us
  blocking collectives: 28.8 us -> 27.8 us
    ppermute x1, waiting for transfers between devices: 1.4 us -> 5.2 us  [local(): rim = lax.ppermute(voltages[:, :RIM], 'tm', [(1, 0), (2, 1), (3, 2)])]
    pallas_call x1, Pallas kernels: 16.1 us -> 12.3 us  [channelize(): pl.pallas_call(channel_kernel, out_shape=jax.ShapeDtypeStruct((128, STN,...]
    mul x4 -> x0, other arithmetic: 3.75 us -> none  [the longest x1 1.64 us: rotations(): return (ac, asn, bc, sine * sign)]
    all_to_all x1, blocking collectives: 28.8 us -> 27.8 us  [local(): received = lax.all_to_all(sent, ('tm', 'stn'), 0, 0, tiled=True)]
  transfers between devices with their start and end apart: 1 -> 1, of which waited for: 1 -> 1; matrix products, arithmetic and copies ran while one was open for 6% -> 0% of each run, Pallas kernels for 0% -> 0%
where the time goes in v2:
time: 58.7 us; the launch traced here: 58.4 us
  blocking collectives  27.8 us (47%)
  Pallas kernels  20.6 us (35%)
  waiting for transfers between devices  5.2 us (9%)
  starting transfers between devices  3.28 us (6%)
  local copies, waits for them, and re-layouts  1.52 us (3%)
    all_to_all x1, blocking collectives, local(): received = lax.all_to_all(sent, ('tm', 'stn'), 0, 0, tiled=True)  27.8 us
    pallas_call x1, Pallas kernels, channelize(): pl.pallas_call(channel_kernel, out_shape=jax.ShapeDtypeStruct((128, STN,...  12.3 us
    pallas_call x1, Pallas kernels, correlate(): pl.pallas_call(correlate_kernel, out_shape=jax.ShapeDtypeStruct((4, 1024,...  8.28 us
    ppermute x1, waiting for transfers between devices, local(): rim = lax.ppermute(voltages[:, :RIM], 'tm', [(1, 0), (2, 1), (3, 2)])  5.2 us
    ppermute x1, starting transfers between devices, local(): rim = lax.ppermute(voltages[:, :RIM], 'tm', [(1, 0), (2, 1), (3, 2)])  3.28 us
  transfers between devices with their start and end apart: 1, of which 1 were waited for; matrix products, arithmetic and copies ran while one was open for 0% of the time, Pallas kernels for 0%

profile of v2, /device:TPU:1, one launch (start us, length us, event | category | flops | bytes accessed | tf_op | source)
XLA Modules:
  0.0 58.4 jit_solution(5190639281135449234)
XLA Ops:
  0.0 0.9 %slice.3 = bf16[32,1536]{1,0:T(8,128)(2,1)S(1)} slice(bf16[32,131072]{1,0:T(8,128)(2,1)} %volt_hbm.1), slice={[0:32], [0:1536]} | slice | bytes 196608 | tf_op jit(solution)/shard_map/slice | solution.py:267
  0.9 3.3 %collective-permute-start = (bf16[32,1536]{1,0:T(8,128)(2,1)S(1)}, bf16[32,1536]{1,0:T(8,128)(2,1)S(1)}, u32[]{:S(2)}, u32[]{:S(2)}) collective-permute-start(bf16[32,1536]{1,0:T(8,128)(2,1)S(1)} %slice.3), channel_id=1, source_target_pairs={{32,0},{64,32},{96,64},{33,1},{65,33},{97,65},{34,2},{66,34},{98,6... | collective-permute-start | bytes 294920 | tf_op jit(solution)/shard_map/ppermute | solution.py:267
  4.2 5.2 %collective-permute-done.rim_ref = bf16[32,1536]{1,0:T(8,128)(2,1)S(1)} collective-permute-done((bf16[32,1536]{1,0:T(8,128)(2,1)S(1)}, bf16[32,1536]{1,0:T(8,128)(2,1)S(1)}, u32[]{:S(2)}, u32[]{:S(2)}) %collective-permute-start) | collective-permute-done | bytes 98336 | tf_op jit(solution)/shard_map/ppermute | solution.py:267
  9.4 0.0 copy-start
  9.4 0.6 %copy-done = bf16[32,1536]{1,0:T(8,128)(2,1)} copy-done((bf16[32,1536]{1,0:T(8,128)(2,1)}, bf16[32,1536]{1,0:T(8,128)(2,1)S(1)}, u32[]{:S(2)}) %copy-start) | copy-done | bytes 98328
  10.0 12.3 %channelize.1 = bf16[128,32,128]{2,1,0:T(8,128)(2,1)} custom-call(bf16[32,131072]{1,0:T(8,128)(2,1)} %volt_hbm.1, bf16[32,1536]{1,0:T(8,128)(2,1)} %copy-done, bf16[1024,256]{1,0:T(8,128)(2,1)} %constant.8.clone.w_ref, bf16[768,256]{1,0:T(8,128)(2,1)} %constant.9.clone.g_ref, bf16[512,512]{1,0:T(8,128)(2,1)} %constant.10.clone.m_ref, s32[1,32]{1,0:T(1,128)} %bitcast.3, ...), custom_call_target="tpu_custom_call" | custom-call | tf_op jit(solution)/shard_map/channelize/pallas_call | solution.py:182
  22.3 27.8 %all_to_all.5.r_ref = bf16[128,32,128]{2,1,0:T(8,128)(2,1)} all-to-all(bf16[128,32,128]{2,1,0:T(8,128)(2,1)} %channelize.1), channel_id=1, replica_groups=mesh['tm'=4,'stn'=32] {'tm','stn'}, dimensions={0} | all-to-all | bytes 2097152 | tf_op jit(solution)/shard_map/all_to_all | solution.py:269
  50.1 8.3 %correlate.1 = f32[4,1024,1024]{2,1,0:T(8,128)} custom-call(bf16[128,32,128]{2,1,0:T(8,128)(2,1)} %all_to_all.5.r_ref, bf16[512,512]{1,0:T(8,128)(2,1)} %constant.11.clone.m_ref), custom_call_target="tpu_custom_call" | custom-call | tf_op jit(solution)/shard_map/correlate/pallas_call | solution.py:251
Async XLA Ops:
  0.9 8.5 %collective-permute-start = (bf16[32,1536]{1,0:T(8,128)(2,1)S(1)}, bf16[32,1536]{1,0:T(8,128)(2,1)S(1)}, u32[]{:S(2)}, u32[]{:S(2)}) collective-permute-start(bf16[32,1536]{1,0:T(8,128)(2,1)S(1)} %slice.3), channel_id=1, source_target_pairs={{32,0},{64,32},{96,64},{33,1},{65,33},{97,65},{34,2},{66,34},{98,6... | collective-permute-start | bytes 294920 | tf_op jit(solution)/shard_map/ppermute | solution.py:267
  9.4 0.6 %copy-start = (bf16[32,1536]{1,0:T(8,128)(2,1)}, bf16[32,1536]{1,0:T(8,128)(2,1)S(1)}, u32[]{:S(2)}) copy-start(bf16[32,1536]{1,0:T(8,128)(2,1)S(1)} %collective-permute-done.rim_ref) | copy-start | bytes 294916

commit v3 on v2

--- a/solution.py
+++ b/solution.py
@@ -19,6 +19,7 @@
 RIM = (TAPS - 1) * NFFT
 CHUNK = 16
 WIDE = 32
+LIMIT = 40 * 2**20
 TURN = NFFT * NFINE
 F32 = jnp.float32
 BF16 = jnp.bfloat16
@@ -67,8 +68,8 @@
     return np.eye(512)[:, source].astype(jnp.bfloat16)
 
 
-def channel_kernel(
-    volt_hbm, rim_ref, w_ref, g_ref, m_ref, d_ref, p_ref, f_ref, out_ref, xbuf, cbuf, dbuf, tcos, tsin, sems
+def coarse_kernel(
+    volt_hbm, w_hbm, d_hbm, p_hbm, f_hbm, cbuf, tcos, tsin, w_ref, xbuf, small, sems, tsems
 ):
     def copy(c):
         width = CHUNK * NFFT
@@ -76,9 +77,18 @@
             volt_hbm.at[:, pl.ds(c * width, width)], xbuf.at[:, pl.ds(c * width, width)], sems.at[c]
         )
 
-    for c in (0, 1, 4, 5, 2, 6, 3, 7, 8, 9, 12, 13, 10, 14, 11, 15):
+    early = (0, 1, 2, 4, 5, 6)
+    late = (3, 7, 8, 9, 10, 12, 13, 14, 11, 15)
+    streams = [
+        pltpu.make_async_copy(source, small.at[k], tsems.at[k]) for k, source in enumerate((d_hbm, p_hbm, f_hbm))
+    ]
+    for each in streams:
+        each.start()
+    weights = pltpu.make_async_copy(w_hbm, w_ref, tsems.at[3])
+    weights.start()
+    for c in early:
         copy(c).start()
-    xbuf[:, FRAMES * NFFT :] = rim_ref[...]
+    xbuf[:, FRAMES * NFFT :] = jnp.zeros((STN, RIM), BF16)
     first_half = lax.broadcasted_iota(jnp.int32, (WIDE * STN, 128), 1) < 64
     diagonal = lax.broadcasted_iota(jnp.int32, (STN, STN), 0) == lax.broadcasted_iota(jnp.int32, (STN, STN), 1)
 
@@ -87,9 +97,11 @@
         picked = jnp.sum(jnp.where(diagonal, spread, 0.0), 1, keepdims=True)
         return jnp.broadcast_to(picked, (STN, 128))
 
-    delay = column(d_ref).astype(jnp.int32)
-    phase = column(p_ref).astype(jnp.int32)
-    keep = column(f_ref) * 0.125
+    for each in streams:
+        each.wait()
+    delay = column(small.at[0]).astype(jnp.int32)
+    phase = column(small.at[1]).astype(jnp.int32)
+    keep = column(small.at[2]) * 0.125
     fine_id = lax.broadcasted_iota(jnp.int32, (STN, 128), 1) // 2 - NFINE // 2
 
     def rotation(band):
@@ -106,9 +118,8 @@
         imag = jnp.where(swap, cosine, sine) * keep
         real = jnp.where(((quarter + 1) & 2) == 2, -real, real)
         imag = jnp.where((quarter & 2) == 2, -imag, imag)
-        row = pl.multiple_of(band * STN, STN)
-        tcos[pl.ds(row, STN), :] = real
-        tsin[pl.ds(row, STN), :] = imag
+        tcos[band] = real
+        tsin[band] = imag
 
     def spectrum(base):
         def frame(j):
@@ -128,12 +139,16 @@
 
         @pl.when(i == 0)
         def _():
-            copy(0).wait()
-
-        @pl.when(part == 0)
+            weights.wait()
+            for c in early:
+                copy(c).wait()
+            for c in late:
+                copy(c).start()
+
+        @pl.when(i == 2)
         def _():
-            for c in (1, 2, 4, 5, 6):
-                copy(a + c).wait()
+            for c in (9, 10, 12, 13, 14):
+                copy(c).wait()
 
         @pl.when(part == 1)
         def _():
@@ -151,58 +166,120 @@
         for j in range(8):
             rotation(i * 8 + j)
 
-    for sb in range(4):
-        streams = jnp.swapaxes(cbuf[:, sb * 8 : (sb + 1) * 8, :], 0, 1)
-        turned = jnp.stack([streams[s].T for s in range(8)], 0)
-        dbuf[:, sb * 8 : (sb + 1) * 8, :] = jnp.swapaxes(turned, 0, 1)
-
-    per = 16
-    rows = per * STN
-    for h in range(BANDS // per):
+
+def fine_kernel(
+    c_ref, rim_ref, w_ref, tcos, tsin, g_hbm, m_hbm, out_hbm, g_ref, m_ref, dbuf0, dbuf1, obuf0, obuf1, tsems
+):
+    tables = [
+        pltpu.make_async_copy(source, target, tsems.at[k])
+        for k, (source, target) in enumerate(((g_hbm, g_ref), (m_hbm, m_ref)))
+    ]
+    tables[0].start()
+    tables[1].start()
+    none = jnp.zeros((STN, NFFT), BF16)
+    rim = [rim_ref[:, k * NFFT : (k + 1) * NFFT] for k in range(TAPS - 1)]
+    left = jnp.concatenate([none, none, none, rim[0]], 0)
+    right = jnp.concatenate([none] + rim, 0)
+    z = jnp.dot(jnp.concatenate([left, right], 1), w_ref[...], preferred_element_type=F32)
+    y = z[: 3 * STN, :128] + z[STN:, 128:]
+    second_half = lax.broadcasted_iota(jnp.int32, (3 * STN, 128), 1) >= 64
+    extra = jnp.where(second_half, y + pltpu.roll(y, 64, 1), 0.0).reshape(3, STN, 128)
+    last = 2 * NFINE - 3
+    part = STN // 2
+    rows = BANDS * part
+
+    def reorder(h, dbuf):
+        for sb in range(2):
+            start = h * part + sb * 8
+            ending = c_ref[last:, start : start + 8, :] + extra[:, start : start + 8, :]
+            block = jnp.concatenate([c_ref[:last, start : start + 8, :], ending], 0)
+            streams = jnp.swapaxes(block, 0, 1)
+            turned = jnp.stack([streams[s].T for s in range(8)], 0)
+            dbuf[:, sb * 8 : (sb + 1) * 8, :] = jnp.swapaxes(turned, 0, 1)
+
+    def finish(h, dbuf, obuf):
         reals, imags = [], []
-        cosine = tcos[h * rows : (h + 1) * rows, :]
-        sine = tsin[h * rows : (h + 1) * rows, :]
+        cosine = tcos[:, h * part : (h + 1) * part, :].reshape(rows, 128)
+        sine = tsin[:, h * part : (h + 1) * part, :].reshape(rows, 128)
         for p in range(2):
-            starts = [(p * 2 + q) * BANDS + h * per for q in range(2)]
-            data = jnp.concatenate([dbuf[x : x + per].reshape(rows, 128) for x in starts], 1)
+            starts = [(p * 2 + q) * BANDS for q in range(2)]
+            data = jnp.concatenate([dbuf[x : x + BANDS].reshape(rows, 128) for x in starts], 1)
             high = data.astype(BF16)
             low = (data - high.astype(F32)).astype(BF16)
             z = jnp.dot(jnp.concatenate([high, low, high], 1), g_ref[...], preferred_element_type=F32)
             reals.append((z[:, :128] * cosine + z[:, 128:] * sine).astype(BF16))
             imags.append((z[:, 128:] * cosine - z[:, :128] * sine).astype(BF16))
         moved = jnp.dot(jnp.concatenate(reals + imags, 1), m_ref[...], preferred_element_type=F32).astype(BF16)
-        for j in range(per):
+        for j in range(BANDS):
             for kh in range(4):
-                out_ref[(h * per + j) * 4 + kh] = moved[j * STN : (j + 1) * STN, kh * 128 : (kh + 1) * 128]
+                obuf[j * 4 + kh] = moved[j * part : (j + 1) * part, kh * 128 : (kh + 1) * 128]
+
+    def send(h, obuf):
+        return pltpu.make_async_copy(obuf, out_hbm.at[:, pl.ds(h * part, part), :], tsems.at[2 + h])
+
+    reorder(0, dbuf0)
+    reorder(1, dbuf1)
+    tables[0].wait()
+    tables[1].wait()
+    finish(0, dbuf0, obuf0)
+    send(0, obuf0).start()
+    finish(1, dbuf1, obuf1)
+    send(1, obuf1).start()
+    send(0, obuf0).wait()
+    send(1, obuf1).wait()
 
 
 def channelize(voltages, rim, delays, phases, flags):
     vm = pl.BlockSpec(memory_space=pltpu.VMEM)
     hbm = pl.BlockSpec(memory_space=pl.ANY)
-    return pl.pallas_call(
-        channel_kernel,
-        out_shape=jax.ShapeDtypeStruct((128, STN, 128), BF16),
-        in_specs=[hbm] + [vm] * 7,
-        out_specs=vm,
+    limits = pltpu.CompilerParams(vmem_limit_bytes=LIMIT)
+
+    def near(array):
+        return pltpu.with_memory_space_constraint(array, pltpu.VMEM)
+
+    def far(array):
+        return pltpu.with_memory_space_constraint(array, pltpu.HBM)
+
+    block = pltpu.VMEM((2 * NFINE, STN, 128), F32)
+    table = pltpu.VMEM((BANDS, STN, 128), F32)
+    coarse, tcos, tsin, weights = pl.pallas_call(
+        coarse_kernel,
+        out_shape=[block, table, table, pltpu.VMEM((1024, 256), BF16)],
+        in_specs=[hbm] * 5,
+        out_specs=[vm] * 4,
         scratch_shapes=[
             pltpu.VMEM((STN, FRAMES * NFFT + RIM), BF16),
-            pltpu.VMEM((2 * NFINE, STN, 128), F32),
-            pltpu.VMEM((128, STN, 128), F32),
-            pltpu.VMEM((BANDS * STN, 128), F32),
-            pltpu.VMEM((BANDS * STN, 128), F32),
+            pltpu.VMEM((3, 1, STN), jnp.int32),
             pltpu.SemaphoreType.DMA((16,)),
+            pltpu.SemaphoreType.DMA((4,)),
         ],
-        name="channelize",
+        compiler_params=limits,
+        name="coarse",
     )(
-        voltages,
-        rim,
-        jnp.asarray(coarse_weights()),
-        jnp.asarray(fine_weights()),
-        jnp.asarray(send_moves()),
-        delays.reshape(1, STN),
-        phases.reshape(1, STN),
-        flags.reshape(1, STN),
+        far(voltages),
+        far(jnp.asarray(coarse_weights())),
+        far(delays.reshape(1, STN)),
+        far(phases.reshape(1, STN)),
+        far(flags.reshape(1, STN)),
     )
+    half = (128, STN // 2, 128)
+    return pl.pallas_call(
+        fine_kernel,
+        out_shape=jax.ShapeDtypeStruct((128, STN, 128), BF16),
+        in_specs=[vm] * 5 + [hbm, hbm],
+        out_specs=hbm,
+        scratch_shapes=[
+            pltpu.VMEM((768, 256), BF16),
+            pltpu.VMEM((512, 512), BF16),
+            pltpu.VMEM(half, F32),
+            pltpu.VMEM(half, F32),
+            pltpu.VMEM(half, BF16),
+            pltpu.VMEM(half, BF16),
+            pltpu.SemaphoreType.DMA((4,)),
+        ],
+        compiler_params=limits,
+        name="fine",
+    )(near(coarse), near(rim), near(weights), near(tcos), near(tsin), far(jnp.asarray(fine_weights())), far(jnp.asarray(send_moves())))
 
 
 def correlate_kernel(r_ref, m_ref, out_hbm, x_buf, s_buf, o_buf, sems):

time: 58.7 us -> 54.7 us (0.932)
  waiting for transfers between devices: 5.2 us -> 0.01 us
  blocking collectives: 27.8 us -> 30 us
  local copies, waits for them, and re-layouts: 1.52 us -> 0.9 us
    ppermute x1, waiting for transfers between devices: 5.2 us -> 0.01 us  [local(): rim = lax.ppermute(voltages[:, :RIM], 'tm', [(1, 0), (2, 1), (3, 2)])]
    all_to_all x1, blocking collectives: 27.8 us -> 30 us  [local(): received = lax.all_to_all(sent, ('tm', 'stn'), 0, 0, tiled=True)]
    unnamed x2 -> x0, local copies, waits for them, and re-layouts: 0.62 us -> none
    pallas_call x1 -> x2, Pallas kernels: 12.3 us -> 12 us  [the longest x1 7.84 us: channelize(): pl.pallas_call(coarse_kernel, out_shape=[block, table, table, pltpu.VMEM(...]
  transfers between devices with their start and end apart: 1 -> 1, of which waited for: 1 -> 0; matrix products, arithmetic and copies ran while one was open for 0% -> 0% of each run, Pallas kernels for 0% -> 14%
where the time goes in v3:
time: 54.7 us; the launch traced here: 54.5 us
  blocking collectives  30 us (55%)
  Pallas kernels  20.3 us (37%)
  starting transfers between devices  3.28 us (6%)
  local copies, waits for them, and re-layouts  0.9 us (2%)
    all_to_all x1, blocking collectives, local(): received = lax.all_to_all(sent, ('tm', 'stn'), 0, 0, tiled=True)  30 us
    pallas_call x1, Pallas kernels, correlate(): pl.pallas_call(correlate_kernel, out_shape=jax.ShapeDtypeStruct((4, 1024,...  8.28 us
    pallas_call x1, Pallas kernels, channelize(): pl.pallas_call(coarse_kernel, out_shape=[block, table, table, pltpu.VMEM(...  7.84 us
    pallas_call x1, Pallas kernels, channelize(): pl.pallas_call(fine_kernel, out_shape=jax.ShapeDtypeStruct((128, STN, 128...  4.19 us
    ppermute x1, starting transfers between devices, local(): rim = lax.ppermute(voltages[:, :RIM], 'tm', [(1, 0), (2, 1), (3, 2)])  3.28 us
  transfers between devices with their start and end apart: 1, of which 0 were waited for; matrix products, arithmetic and copies ran while one was open for 0% of the time, Pallas kernels for 14%

profile of v3, /device:TPU:1, one launch (start us, length us, event | category | flops | bytes accessed | tf_op | source)
XLA Modules:
  0.0 54.5 jit_solution(898678782581084012)
XLA Ops:
  0.0 0.9 %slice.3 = bf16[32,1536]{1,0:T(8,128)(2,1)S(1)} slice(bf16[32,131072]{1,0:T(8,128)(2,1)} %volt_hbm.1), slice={[0:32], [0:1536]} | slice | bytes 196608 | tf_op jit(solution)/shard_map/slice | solution.py:344
  0.9 3.3 %collective-permute-start = (bf16[32,1536]{1,0:T(8,128)(2,1)S(1)}, bf16[32,1536]{1,0:T(8,128)(2,1)S(1)}, u32[]{:S(2)}, u32[]{:S(2)}) collective-permute-start(bf16[32,1536]{1,0:T(8,128)(2,1)S(1)} %slice.3), channel_id=1, source_target_pairs={{32,0},{64,32},{96,64},{33,1},{65,33},{97,65},{34,2},{66,34},{98,6... | collective-permute-start | bytes 294920 | tf_op jit(solution)/shard_map/ppermute | solution.py:344
  4.2 7.8 %coarse.1 = (f32[128,32,128]{2,1,0:T(8,128)S(1)}, f32[32,32,128]{2,1,0:T(8,128)S(1)}, f32[32,32,128]{2,1,0:T(8,128)S(1)}, bf16[1024,256]{1,0:T(8,128)(2,1)S(1)}) custom-call(bf16[32,131072]{1,0:T(8,128)(2,1)} %volt_hbm.1, bf16[1024,256]{1,0:T(8,128)(2,1)} %constant.8.clone.w_hbm, s32[1,32]{1,0:T(1,128)} %bitcast.3, s32[1,32]{1,0:T(1,128)} %bitcast.4, ...), custom_call_target="tpu_custom_call" | custom-call | tf_op jit(solution)/shard_map/coarse/pallas_call | solution.py:245
  12.0 0.0 collective-permute-done.rim_ref
  12.0 4.2 %fine.1 = bf16[128,32,128]{2,1,0:T(8,128)(2,1)S(1)} custom-call(f32[128,32,128]{2,1,0:T(8,128)S(1)} %get-tuple-element.9.c_ref, bf16[32,1536]{1,0:T(8,128)(2,1)S(1)} %collective-permute-done.rim_ref, bf16[1024,256]{1,0:T(8,128)(2,1)S(1)} %get-tuple-element.10.w_ref, f32[32,32,128]{2,1,0:T(8,128)S(1)} %get-tuple-element.11.tcos, ...), custom_call_target="tpu_custom_call" | custom-call | tf_op jit(solution)/shard_map/fine/pallas_call | solution.py:266
  16.2 30.0 %all_to_all.5.r_ref = bf16[128,32,128]{2,1,0:T(8,128)(2,1)} all-to-all(bf16[128,32,128]{2,1,0:T(8,128)(2,1)S(1)} %fine.1), channel_id=1, replica_groups=mesh['tm'=4,'stn'=32] {'tm','stn'}, dimensions={0} | all-to-all | bytes 2097152 | tf_op jit(solution)/shard_map/all_to_all | solution.py:346
  46.2 8.3 %correlate.1 = f32[4,1024,1024]{2,1,0:T(8,128)} custom-call(bf16[128,32,128]{2,1,0:T(8,128)(2,1)} %all_to_all.5.r_ref, bf16[512,512]{1,0:T(8,128)(2,1)} %constant.11.clone.m_ref), custom_call_target="tpu_custom_call" | custom-call | tf_op jit(solution)/shard_map/correlate/pallas_call | solution.py:328
Async XLA Ops:
  0.9 11.1 %collective-permute-start = (bf16[32,1536]{1,0:T(8,128)(2,1)S(1)}, bf16[32,1536]{1,0:T(8,128)(2,1)S(1)}, u32[]{:S(2)}, u32[]{:S(2)}) collective-permute-start(bf16[32,1536]{1,0:T(8,128)(2,1)S(1)} %slice.3), channel_id=1, source_target_pairs={{32,0},{64,32},{96,64},{33,1},{65,33},{97,65},{34,2},{66,34},{98,6... | collective-permute-start | bytes 294920 | tf_op jit(solution)/shard_map/ppermute | solution.py:344

commit v4 on v3

--- a/solution.py
+++ b/solution.py
@@ -25,6 +25,14 @@
 BF16 = jnp.bfloat16
 
 
+def near(array):
+    return pltpu.with_memory_space_constraint(array, pltpu.VMEM)
+
+
+def far(array):
+    return pltpu.with_memory_space_constraint(array, pltpu.HBM)
+
+
 def split_two(table):
     high = table.astype(jnp.bfloat16)
     low = (table - high.astype(np.float64)).astype(jnp.bfloat16)
@@ -68,27 +76,30 @@
     return np.eye(512)[:, source].astype(jnp.bfloat16)
 
 
-def coarse_kernel(
-    volt_hbm, w_hbm, d_hbm, p_hbm, f_hbm, cbuf, tcos, tsin, w_ref, xbuf, small, sems, tsems
-):
-    def copy(c):
-        width = CHUNK * NFFT
-        return pltpu.make_async_copy(
-            volt_hbm.at[:, pl.ds(c * width, width)], xbuf.at[:, pl.ds(c * width, width)], sems.at[c]
-        )
-
-    early = (0, 1, 2, 4, 5, 6)
-    late = (3, 7, 8, 9, 10, 12, 13, 14, 11, 15)
-    streams = [
-        pltpu.make_async_copy(source, small.at[k], tsems.at[k]) for k, source in enumerate((d_hbm, p_hbm, f_hbm))
-    ]
-    for each in streams:
+def frames_copy(volt_hbm, xbuf, sem, start, count):
+    where = pl.ds(start * NFFT, count * NFFT)
+    return pltpu.make_async_copy(volt_hbm.at[:, where], xbuf.at[:, where], sem)
+
+
+def first_kernel(volt_hbm, w_hbm, d_hbm, p_hbm, f_hbm, rim_ref, xbuf, w_ref, small, sems):
+    copies = [pltpu.make_async_copy(volt_hbm.at[:, pl.ds(0, RIM)], rim_ref, sems.at[0])]
+    for k, source in enumerate((d_hbm, p_hbm, f_hbm)):
+        copies.append(pltpu.make_async_copy(source, small.at[k], sems.at[1 + k]))
+    for k, start in enumerate((0, NFINE)):
+        copies.append(frames_copy(volt_hbm, xbuf, sems.at[4 + k], start, WIDE + 3))
+    copies.append(pltpu.make_async_copy(w_hbm, w_ref, sems.at[6]))
+    for each in copies:
         each.start()
-    weights = pltpu.make_async_copy(w_hbm, w_ref, tsems.at[3])
-    weights.start()
-    for c in early:
-        copy(c).start()
     xbuf[:, FRAMES * NFFT :] = jnp.zeros((STN, RIM), BF16)
+    for each in copies:
+        each.wait()
+
+
+def coarse_kernel(volt_hbm, x_in, w_ref, small, cbuf, tcos, tsin, xbuf, sems):
+    segments = ((35, 29), (99, 32), (131, 32), (192, 35), (163, 29), (227, 29))
+    copies = [frames_copy(volt_hbm, xbuf, sems.at[k], *segment) for k, segment in enumerate(segments)]
+    for each in copies:
+        each.start()
     first_half = lax.broadcasted_iota(jnp.int32, (WIDE * STN, 128), 1) < 64
     diagonal = lax.broadcasted_iota(jnp.int32, (STN, STN), 0) == lax.broadcasted_iota(jnp.int32, (STN, STN), 1)
 
@@ -97,8 +108,6 @@
         picked = jnp.sum(jnp.where(diagonal, spread, 0.0), 1, keepdims=True)
         return jnp.broadcast_to(picked, (STN, 128))
 
-    for each in streams:
-        each.wait()
     delay = column(small.at[0]).astype(jnp.int32)
     phase = column(small.at[1]).astype(jnp.int32)
     keep = column(small.at[2]) * 0.125
@@ -137,27 +146,12 @@
         part = i % 2
         a = (i // 2) * 8 + part * 2
 
-        @pl.when(i == 0)
-        def _():
-            weights.wait()
-            for c in early:
-                copy(c).wait()
-            for c in late:
-                copy(c).start()
-
-        @pl.when(i == 2)
-        def _():
-            for c in (9, 10, 12, 13, 14):
-                copy(c).wait()
-
-        @pl.when(part == 1)
-        def _():
-            for c in (1, 5):
-                copy(a + c).wait()
-
-        @pl.when(i == 1)
-        def _():
-            copy(8).wait()
+        for k in range(3):
+
+            @pl.when(i == k + 1)
+            def _():
+                copies[2 * k].wait()
+                copies[2 * k + 1].wait()
 
         y0 = spectrum(a * CHUNK)
         y1 = spectrum((a + 4) * CHUNK)
@@ -217,11 +211,11 @@
     def send(h, obuf):
         return pltpu.make_async_copy(obuf, out_hbm.at[:, pl.ds(h * part, part), :], tsems.at[2 + h])
 
-    reorder(0, dbuf0)
-    reorder(1, dbuf1)
     tables[0].wait()
     tables[1].wait()
+    reorder(0, dbuf0)
     finish(0, dbuf0, obuf0)
+    reorder(1, dbuf1)
     send(0, obuf0).start()
     finish(1, dbuf1, obuf1)
     send(1, obuf1).start()
@@ -229,32 +223,27 @@
     send(1, obuf1).wait()
 
 
-def channelize(voltages, rim, delays, phases, flags):
+def channelize(voltages, delays, phases, flags):
     vm = pl.BlockSpec(memory_space=pltpu.VMEM)
     hbm = pl.BlockSpec(memory_space=pl.ANY)
     limits = pltpu.CompilerParams(vmem_limit_bytes=LIMIT)
 
-    def near(array):
-        return pltpu.with_memory_space_constraint(array, pltpu.VMEM)
-
-    def far(array):
-        return pltpu.with_memory_space_constraint(array, pltpu.HBM)
-
     block = pltpu.VMEM((2 * NFINE, STN, 128), F32)
     table = pltpu.VMEM((BANDS, STN, 128), F32)
-    coarse, tcos, tsin, weights = pl.pallas_call(
-        coarse_kernel,
-        out_shape=[block, table, table, pltpu.VMEM((1024, 256), BF16)],
+    frames = pltpu.VMEM((STN, FRAMES * NFFT + RIM), BF16)
+    rim, begun, weights, small = pl.pallas_call(
+        first_kernel,
+        out_shape=[
+            pltpu.VMEM((STN, RIM), BF16),
+            frames,
+            pltpu.VMEM((1024, 256), BF16),
+            pltpu.VMEM((3, 1, STN), jnp.int32),
+        ],
         in_specs=[hbm] * 5,
         out_specs=[vm] * 4,
-        scratch_shapes=[
-            pltpu.VMEM((STN, FRAMES * NFFT + RIM), BF16),
-            pltpu.VMEM((3, 1, STN), jnp.int32),
-            pltpu.SemaphoreType.DMA((16,)),
-            pltpu.SemaphoreType.DMA((4,)),
-        ],
+        scratch_shapes=[pltpu.SemaphoreType.DMA((7,))],
         compiler_params=limits,
-        name="coarse",
+        name="first",
     )(
         far(voltages),
         far(jnp.asarray(coarse_weights())),
@@ -262,6 +251,17 @@
         far(phases.reshape(1, STN)),
         far(flags.reshape(1, STN)),
     )
+    rim = lax.ppermute(rim, "tm", [(1, 0), (2, 1), (3, 2)])
+    coarse, tcos, tsin, _ = pl.pallas_call(
+        coarse_kernel,
+        out_shape=[block, table, table, frames],
+        in_specs=[hbm, vm, vm, vm],
+        out_specs=[vm] * 4,
+        scratch_shapes=[pltpu.SemaphoreType.DMA((6,))],
+        input_output_aliases={1: 3},
+        compiler_params=limits,
+        name="coarse",
+    )(far(voltages), near(begun), near(weights), near(small))
     half = (128, STN // 2, 128)
     return pl.pallas_call(
         fine_kernel,
@@ -336,13 +336,13 @@
             pltpu.VMEM((4, 1024, 1024), F32),
             pltpu.SemaphoreType.DMA((4, 4)),
         ],
+        compiler_params=pltpu.CompilerParams(vmem_limit_bytes=LIMIT),
         name="correlate",
-    )(received, jnp.asarray(group_moves()))
+    )(near(received), near(jnp.asarray(group_moves())))
 
 
 def local(voltages, delays, phases, flags):
-    rim = lax.ppermute(voltages[:, :RIM], "tm", [(1, 0), (2, 1), (3, 2)])
-    sent = channelize(voltages, rim, delays, phases, flags)
+    sent = channelize(voltages, delays, phases, flags)
     received = lax.all_to_all(sent, ("tm", "stn"), 0, 0, tiled=True)
     return correlate(received)
 

time: 54.7 us -> 51.8 us (0.947)
  Pallas kernels: 20.3 us -> 18.4 us
  local copies, waits for them, and re-layouts: 0.9 us -> 0.01 us
    pallas_call x1, Pallas kernels: 8.28 us -> 6.92 us  [correlate(): pl.pallas_call(correlate_kernel, out_shape=jax.ShapeDtypeStruct((4, 1024,...]
    slice x1 -> x0, local copies, waits for them, and re-layouts: 0.9 us -> none  [local(): rim = lax.ppermute(voltages[:, :RIM], 'tm', [(1, 0), (2, 1), (3, 2)])]
    pallas_call x1 -> x2, Pallas kernels: 7.84 us -> 7.67 us  [the longest x1 5.77 us: channelize(): pl.pallas_call(coarse_kernel, out_shape=[block, table, table, frames], in...]
  transfers between devices with their start and end apart: 1 -> 1, of which waited for: 0 -> 0; matrix products, arithmetic and copies ran while one was open for 0% -> 0% of each run, Pallas kernels for 14% -> 11%
where the time goes in v4:
time: 51.8 us; the launch traced here: 51.6 us
  blocking collectives  29.9 us (58%)
  Pallas kernels  18.4 us (36%)
  starting transfers between devices  3.29 us (6%)
    all_to_all x1, blocking collectives, local(): received = lax.all_to_all(sent, ('tm', 'stn'), 0, 0, tiled=True)  29.9 us
    pallas_call x1, Pallas kernels, correlate(): pl.pallas_call(correlate_kernel, out_shape=jax.ShapeDtypeStruct((4, 1024,...  6.92 us
    pallas_call x1, Pallas kernels, channelize(): pl.pallas_call(coarse_kernel, out_shape=[block, table, table, frames], in...  5.77 us
    pallas_call x1, Pallas kernels, channelize(): pl.pallas_call(fine_kernel, out_shape=jax.ShapeDtypeStruct((128, STN, 128...  3.82 us
    ppermute x1, starting transfers between devices, channelize(): rim = lax.ppermute(rim, 'tm', [(1, 0), (2, 1), (3, 2)])  3.29 us
    pallas_call x1, Pallas kernels, channelize(): pl.pallas_call(first_kernel, out_shape=[pltpu.VMEM((STN, RIM), BF16), fra...  1.9 us
  transfers between devices with their start and end apart: 1, of which 0 were waited for; matrix products, arithmetic and copies ran while one was open for 0% of the time, Pallas kernels for 11%

profile of v4, /device:TPU:1, one launch (start us, length us, event | category | flops | bytes accessed | tf_op | source)
XLA Modules:
  0.0 51.6 jit_solution(10243333100432820837)
XLA Ops:
  0.0 1.9 %first.1 = (bf16[32,1536]{1,0:T(8,128)(2,1)S(1)}, bf16[32,132608]{1,0:T(8,128)(2,1)S(1)}, bf16[1024,256]{1,0:T(8,128)(2,1)S(1)}, s32[3,1,32]{2,1,0:T(1,128)S(1)}) custom-call(bf16[32,131072]{1,0:T(8,128)(2,1)} %volt_hbm.3, bf16[1024,256]{1,0:T(8,128)(2,1)} %constant.8.clone.w_hbm, s32[1,32]{1,0:T(1,128)} %bitcast.3, s32[1,32]{1,0:T(1,128)} %bitcast.4, ...), custom_call_target="tpu_custom_call" | custom-call | tf_op jit(solution)/shard_map/first/pallas_call | solution.py:234
  1.9 3.3 %collective-permute-start = (bf16[32,1536]{1,0:T(8,128)(2,1)S(1)}, bf16[32,1536]{1,0:T(8,128)(2,1)S(1)}, u32[]{:S(2)}, u32[]{:S(2)}) collective-permute-start(bf16[32,1536]{1,0:T(8,128)(2,1)S(1)} %get-tuple-element.16), channel_id=1, source_target_pairs={{32,0},{64,32},{96,64},{33,1},{65,33},{97,65},{34,2},{66,34},{98,6... | collective-permute-start | bytes 294920 | tf_op jit(solution)/shard_map/ppermute | solution.py:254
  5.2 0.0 copy-start
  5.2 5.8 %coarse.1 = (f32[128,32,128]{2,1,0:T(8,128)S(1)}, f32[32,32,128]{2,1,0:T(8,128)S(1)}, f32[32,32,128]{2,1,0:T(8,128)S(1)}, bf16[32,132608]{1,0:T(8,128)(2,1)S(1)}) custom-call(bf16[32,131072]{1,0:T(8,128)(2,1)} %volt_hbm.3, bf16[32,132608]{1,0:T(8,128)(2,1)S(1)} %get-tuple-element.12.x_in, ...), custom_call_target="tpu_custom_call", output_to_operand_aliasing={{3}: (1, {})} | custom-call | tf_op jit(solution)/shard_map/coarse/pallas_call | solution.py:255
  11.0 0.0 collective-permute-done.rim_ref
  11.0 3.8 %fine.1 = bf16[128,32,128]{2,1,0:T(8,128)(2,1)S(1)} custom-call(f32[128,32,128]{2,1,0:T(8,128)S(1)} %get-tuple-element.15.c_ref, bf16[32,1536]{1,0:T(8,128)(2,1)S(1)} %collective-permute-done.rim_ref, bf16[1024,256]{1,0:T(8,128)(2,1)S(1)} %get-tuple-element.13.w_ref, f32[32,32,128]{2,1,0:T(8,128)S(1)} %get-tuple-element.17.tcos, ...), custom_call_target="tpu_custom_call" | custom-call | tf_op jit(solution)/shard_map/fine/pallas_call | solution.py:266
  14.8 29.9 %all_to_all.5.r_ref = bf16[128,32,128]{2,1,0:T(8,128)(2,1)S(1)} all-to-all(bf16[128,32,128]{2,1,0:T(8,128)(2,1)S(1)} %fine.1), channel_id=1, replica_groups=mesh['tm'=4,'stn'=32] {'tm','stn'}, dimensions={0} | all-to-all | bytes 2097152 | tf_op jit(solution)/shard_map/all_to_all | solution.py:346
  44.7 0.0 copy-done
  44.7 6.9 %correlate.1 = f32[4,1024,1024]{2,1,0:T(8,128)} custom-call(bf16[128,32,128]{2,1,0:T(8,128)(2,1)S(1)} %all_to_all.5.r_ref, bf16[512,512]{1,0:T(8,128)(2,1)S(1)} %copy-done), custom_call_target="tpu_custom_call" | custom-call | tf_op jit(solution)/shard_map/correlate/pallas_call | solution.py:328
Async XLA Ops:
  1.9 9.1 %collective-permute-start = (bf16[32,1536]{1,0:T(8,128)(2,1)S(1)}, bf16[32,1536]{1,0:T(8,128)(2,1)S(1)}, u32[]{:S(2)}, u32[]{:S(2)}) collective-permute-start(bf16[32,1536]{1,0:T(8,128)(2,1)S(1)} %get-tuple-element.16), channel_id=1, source_target_pairs={{32,0},{64,32},{96,64},{33,1},{65,33},{97,65},{34,2},{66,34},{98,6... | collective-permute-start | bytes 294920 | tf_op jit(solution)/shard_map/ppermute | solution.py:254
  5.2 39.5 %copy-start = (bf16[512,512]{1,0:T(8,128)(2,1)S(1)}, bf16[512,512]{1,0:T(8,128)(2,1)}, u32[]{:S(2)}) copy-start(bf16[512,512]{1,0:T(8,128)(2,1)} %constant.11.clone.m_ref) | copy-start | bytes 1572868

commit v5 on v4

--- a/solution.py
+++ b/solution.py
@@ -211,9 +211,9 @@
     def send(h, obuf):
         return pltpu.make_async_copy(obuf, out_hbm.at[:, pl.ds(h * part, part), :], tsems.at[2 + h])
 
+    reorder(0, dbuf0)
     tables[0].wait()
     tables[1].wait()
-    reorder(0, dbuf0)
     finish(0, dbuf0, obuf0)
     reorder(1, dbuf1)
     send(0, obuf0).start()
@@ -305,20 +305,19 @@
     row = lax.broadcasted_iota(jnp.int32, (256, 256), 0)
     upper = lax.broadcasted_iota(jnp.int32, (256, 256), 1) >= row
     prepare(0)
+    prepare(1)
     for g in range(4):
         for j in range(4):
             low, high = j * 256, (j + 1) * 256
             column = x_buf[g, low:high, :]
-            real = product(x_buf[g, :high, :], column)
-            imag = product(s_buf[g, low:, :], column)
             if j > 0:
-                o_buf[g, :low, low:high] = real[:low]
+                o_buf[g, :low, low:high] = product(x_buf[g, :low, :], column)
             if j < 3:
-                o_buf[g, high:, low:high] = imag[256:]
-            o_buf[g, low:high, low:high] = jnp.where(upper, real[low:], imag[:256])
+                o_buf[g, high:, low:high] = product(s_buf[g, high:, :], column)
+            real = product(x_buf[g, low:high, :], column)
+            imag = product(s_buf[g, low:high, :], column)
+            o_buf[g, low:high, low:high] = jnp.where(upper, real, imag)
             send(g, j).start()
-        if g == 0:
-            prepare(1)
     for g in range(4):
         for j in range(4):
             send(g, j).wait()

time: 51.8 us -> 51.4 us (level)
  no operation moved by 1% of the time
where the time goes in v5:
time: 51.4 us; the launch traced here: 51.2 us
  blocking collectives  29.9 us (58%)
  Pallas kernels  18 us (35%)
  starting transfers between devices  3.29 us (6%)
    all_to_all x1, blocking collectives, local(): received = lax.all_to_all(sent, ('tm', 'stn'), 0, 0, tiled=True)  29.9 us
    pallas_call x1, Pallas kernels, correlate(): pl.pallas_call(correlate_kernel, out_shape=jax.ShapeDtypeStruct((4, 1024,...  6.88 us
    pallas_call x1, Pallas kernels, channelize(): pl.pallas_call(coarse_kernel, out_shape=[block, table, table, frames], in...  5.77 us
    pallas_call x1, Pallas kernels, channelize(): pl.pallas_call(fine_kernel, out_shape=jax.ShapeDtypeStruct((128, STN, 128...  3.41 us
    ppermute x1, starting transfers between devices, channelize(): rim = lax.ppermute(rim, 'tm', [(1, 0), (2, 1), (3, 2)])  3.29 us
    pallas_call x1, Pallas kernels, channelize(): pl.pallas_call(first_kernel, out_shape=[pltpu.VMEM((STN, RIM), BF16), fra...  1.9 us
  transfers between devices with their start and end apart: 1, of which 0 were waited for; matrix products, arithmetic and copies ran while one was open for 0% of the time, Pallas kernels for 11%

profile of v5, /device:TPU:1, one launch (start us, length us, event | category | flops | bytes accessed | tf_op | source)
XLA Modules:
  0.0 51.2 jit_solution(15257123277837538664)
XLA Ops:
  0.0 1.9 %first.1 = (bf16[32,1536]{1,0:T(8,128)(2,1)S(1)}, bf16[32,132608]{1,0:T(8,128)(2,1)S(1)}, bf16[1024,256]{1,0:T(8,128)(2,1)S(1)}, s32[3,1,32]{2,1,0:T(1,128)S(1)}) custom-call(bf16[32,131072]{1,0:T(8,128)(2,1)} %volt_hbm.3, bf16[1024,256]{1,0:T(8,128)(2,1)} %constant.8.clone.w_hbm, s32[1,32]{1,0:T(1,128)} %bitcast.3, s32[1,32]{1,0:T(1,128)} %bitcast.4, ...), custom_call_target="tpu_custom_call" | custom-call | tf_op jit(solution)/shard_map/first/pallas_call | solution.py:234
  1.9 3.3 %collective-permute-start = (bf16[32,1536]{1,0:T(8,128)(2,1)S(1)}, bf16[32,1536]{1,0:T(8,128)(2,1)S(1)}, u32[]{:S(2)}, u32[]{:S(2)}) collective-permute-start(bf16[32,1536]{1,0:T(8,128)(2,1)S(1)} %get-tuple-element.16), channel_id=1, source_target_pairs={{32,0},{64,32},{96,64},{33,1},{65,33},{97,65},{34,2},{66,34},{98,6... | collective-permute-start | bytes 294920 | tf_op jit(solution)/shard_map/ppermute | solution.py:254
  5.2 0.0 copy-start
  5.2 5.8 %coarse.1 = (f32[128,32,128]{2,1,0:T(8,128)S(1)}, f32[32,32,128]{2,1,0:T(8,128)S(1)}, f32[32,32,128]{2,1,0:T(8,128)S(1)}, bf16[32,132608]{1,0:T(8,128)(2,1)S(1)}) custom-call(bf16[32,131072]{1,0:T(8,128)(2,1)} %volt_hbm.3, bf16[32,132608]{1,0:T(8,128)(2,1)S(1)} %get-tuple-element.12.x_in, ...), custom_call_target="tpu_custom_call", output_to_operand_aliasing={{3}: (1, {})} | custom-call | tf_op jit(solution)/shard_map/coarse/pallas_call | solution.py:255
  11.0 0.0 collective-permute-done.rim_ref
  11.0 3.4 %fine.1 = bf16[128,32,128]{2,1,0:T(8,128)(2,1)S(1)} custom-call(f32[128,32,128]{2,1,0:T(8,128)S(1)} %get-tuple-element.15.c_ref, bf16[32,1536]{1,0:T(8,128)(2,1)S(1)} %collective-permute-done.rim_ref, bf16[1024,256]{1,0:T(8,128)(2,1)S(1)} %get-tuple-element.13.w_ref, f32[32,32,128]{2,1,0:T(8,128)S(1)} %get-tuple-element.17.tcos, ...), custom_call_target="tpu_custom_call" | custom-call | tf_op jit(solution)/shard_map/fine/pallas_call | solution.py:266
  14.4 29.9 %all_to_all.5.r_ref = bf16[128,32,128]{2,1,0:T(8,128)(2,1)S(1)} all-to-all(bf16[128,32,128]{2,1,0:T(8,128)(2,1)S(1)} %fine.1), channel_id=1, replica_groups=mesh['tm'=4,'stn'=32] {'tm','stn'}, dimensions={0} | all-to-all | bytes 2097152 | tf_op jit(solution)/shard_map/all_to_all | solution.py:345
  44.3 0.0 copy-done
  44.3 6.9 %correlate.1 = f32[4,1024,1024]{2,1,0:T(8,128)} custom-call(bf16[128,32,128]{2,1,0:T(8,128)(2,1)S(1)} %all_to_all.5.r_ref, bf16[512,512]{1,0:T(8,128)(2,1)S(1)} %copy-done), custom_call_target="tpu_custom_call" | custom-call | tf_op jit(solution)/shard_map/correlate/pallas_call | solution.py:327
Async XLA Ops:
  1.9 9.1 %collective-permute-start = (bf16[32,1536]{1,0:T(8,128)(2,1)S(1)}, bf16[32,1536]{1,0:T(8,128)(2,1)S(1)}, u32[]{:S(2)}, u32[]{:S(2)}) collective-permute-start(bf16[32,1536]{1,0:T(8,128)(2,1)S(1)} %get-tuple-element.16), channel_id=1, source_target_pairs={{32,0},{64,32},{96,64},{33,1},{65,33},{97,65},{34,2},{66,34},{98,6... | collective-permute-start | bytes 294920 | tf_op jit(solution)/shard_map/ppermute | solution.py:254
  5.2 39.1 %copy-start = (bf16[512,512]{1,0:T(8,128)(2,1)S(1)}, bf16[512,512]{1,0:T(8,128)(2,1)}, u32[]{:S(2)}) copy-start(bf16[512,512]{1,0:T(8,128)(2,1)} %constant.11.clone.m_ref) | copy-start | bytes 1572868
